TPU v7x, 512 devices: a whole 4x4x16 slice. The times are simulated.
512 devices in a mesh: dp: 64 (over y, z), mp: 8 (over x, core).
Axes of the slice: x: 4, y: 4, z: 16, core: 2. Of those that a mesh axis runs over, the one named last changes fastest.
Arguments:
- x_in: bfloat16 [25600, 2048], P('dp'), may hold values from -6 to 6
- cotangent: bfloat16 [25600, 7168], P('dp', 'mp'), may hold values from -6 to 6
- w_gate: bfloat16 [2048, 7168], P('dp', 'mp'), may hold values from -0.125 to 0.125
- w_up: bfloat16 [2048, 7168], P('dp', 'mp'), may hold values from -0.125 to 0.125
- send_counts: int32 [64, 64], P('dp'), may hold values from 0 to 4, as said below
- recv_counts: int32 [64, 64], P('dp'), may hold values from 0 to 4, as said below
Outputs:
- grad_x: bfloat16 [25600, 2048], P('dp', 'mp')
- grad_gate: float32 [2048, 7168], P('dp', 'mp')
Inputs may be any that keep to these rules, and one draw needn't show every extreme that they name: `send_counts`: each entry is 0 to 4. A quarter of the indices only send and the rest only receive; one sending index sends 4 rows to every receiver, so its live rows reach 400. recv_counts is the transpose of send_counts.
All inputs are finite; a program needn't handle non-finite values.
Results may differ from a plain program's by a relative error of at most 0.014.
Values may be sent and summed in bfloat16 or wider, within the bound.
A program may use at most 64 MiB of HBM per device.

v0:
```python
import jax
import jax.numpy as jnp
from jax import lax
from jax.sharding import PartitionSpec as P

BAL = 208


def contract_last(left, right):
    return lax.dot_general(
        left, right, (((1,), (1,)), ((), ())), preferred_element_type=jnp.float32
    )


def swiglu_back(x_rows, cot_rows, gate_full, up_full, live_mask):
    gate_val = jnp.dot(x_rows, gate_full, preferred_element_type=jnp.float32)
    up_val = jnp.dot(x_rows, up_full, preferred_element_type=jnp.float32)
    sig = jax.nn.sigmoid(gate_val)
    cot_val = cot_rows.astype(jnp.float32)
    d_gate = jnp.where(
        live_mask[:, None], cot_val * up_val * sig * (1.0 + gate_val * (1.0 - sig)), 0.0
    ).astype(jnp.bfloat16)
    d_up = jnp.where(live_mask[:, None], cot_val * gate_val * sig, 0.0).astype(jnp.bfloat16)
    partial_value = contract_last(d_gate, gate_full) + contract_last(d_up, up_full)
    return (partial_value, d_gate)


def group_sum(partial_value):
    return lax.psum_scatter(
        partial_value.astype(jnp.bfloat16), "mp", scatter_dimension=1, tiled=True
    )


def on_device(x_in, cotangent, w_gate, w_up, send_counts, recv_counts):
    rows_cap = x_in.shape[0]
    width = x_in.shape[1]
    dev_count = lax.axis_size("dp")
    gate_full, up_full = (
        lax.all_gather(w_gate, "dp", axis=0, tiled=True),
        lax.all_gather(w_up, "dp", axis=0, tiled=True),
    )
    sent = send_counts[0]
    got = recv_counts[0]
    live_rows = BAL + jnp.sum(sent) - jnp.sum(got)
    live_mask = jnp.arange(rows_cap) < live_rows
    partial_value, d_gate = swiglu_back(x_in, cotangent, gate_full, up_full, live_mask)
    grad_x = group_sum(partial_value)
    block_rows = width // dev_count
    whole = lax.dot_general(
        x_in, d_gate, (((0,), (0,)), ((), ())), preferred_element_type=jnp.float32
    )
    grad_gate = lax.psum_scatter(
        whole.astype(jnp.bfloat16), "dp", scatter_dimension=0, tiled=True
    ).astype(jnp.float32)
    return (grad_x, grad_gate)


def solution(mesh):
    return jax.shard_map(
        on_device,
        mesh=mesh,
        in_specs=(
            P("dp", None),
            P("dp", "mp"),
            P("dp", "mp"),
            P("dp", "mp"),
            P("dp", None),
            P("dp", None),
        ),
        out_specs=(P("dp", "mp"), P("dp", "mp")),
        check_vma=False,
    )
```

profile of v0, /device:TPU:8, one launch (start us, length us, event | category | flops | bytes accessed | tf_op | source)
XLA Modules:
  0.0 1060.5 jit_solution(8219626550588682840)
XLA Ops:
  7.2 0.0 copy-start
  7.2 0.0 all-gather.5.cloned.1.call-start
  7.2 0.7 all-gather.5.cloned.1.call-update
  7.9 0.0 all-gather.3.cloned.1.call-start
  8.0 0.7 all-gather.3.cloned.1.call-update
  8.7 0.0 reduce-scatter.7.cloned.1.call-start
  8.7 1.3 reduce_sum.19
  10.0 1.3 reduce_sum.18
  12.6 0.0 copy-start.2
  12.6 147.1 %all-gather.5.cloned.1.call-done = bf16[2048,896]{1,0:T(8,128)(2,1)} async-done(((bf16[32,896]{1,0:T(8,128)(2,1)}), bf16[2048,896]{1,0:T(8,128)(2,1)}) %all-gather.5.cloned.1.call-update) | async-done | bytes 3670032 | tf_op jit(solution)/shard_map/all_gather | solution.py:39
  159.7 5.0 fusion.11
  164.7 137.7 %all-gather.3.cloned.1.call-done = bf16[2048,896]{1,0:T(8,128)(2,1)} async-done(((bf16[32,896]{1,0:T(8,128)(2,1)}), bf16[2048,896]{1,0:T(8,128)(2,1)}) %all-gather.3.cloned.1.call-update) | async-done | bytes 3670032 | tf_op jit(solution)/shard_map/all_gather | solution.py:40
  302.4 4.6 select_convert_fusion
  307.0 4.0 convert_bitcast_fusion
  311.0 6.1 copy.10
  317.1 0.0 reduce-scatter.7.cloned.1.call-update
  317.2 0.0 reduce-scatter.5.cloned.1.call-start
  317.2 4.1 fusion.12
  321.3 3.1 add_convert_fusion
  324.5 0.0 reduce-scatter.5.cloned.1.call-update
  324.5 687.3 %reduce-scatter.7.cloned.1.call-done = bf16[32,896]{1,0:T(8,128)(2,1)} async-done(((bf16[2048,896]{1,0:T(8,128)(2,1)}), bf16[32,896]{1,0:T(8,128)(2,1)}) %reduce-scatter.7.cloned.1.call-update) | async-done | bytes 57360
  1011.7 1.0 copy.11
  1012.7 0.8 copy.9
  1013.5 40.4 %reduce-scatter.5.cloned.1.call-done = bf16[400,256]{1,0:T(8,128)(2,1)} async-done(((bf16[400,2048]{1,0:T(8,128)(2,1)}), bf16[400,256]{1,0:T(8,128)(2,1)}) %reduce-scatter.5.cloned.1.call-update) | async-done | bytes 204816 | tf_op jit(solution)/shard_map/reduce_scatter | solution.py:29
  (7 shorter events, 0.0 us)
Async XLA Ops:
  7.2 152.6 %copy-start = (bf16[400,2048]{1,0:T(8,128)(2,1)S(1)}, bf16[400,2048]{1,0:T(8,128)(2,1)}, u32[]{:S(2)}) copy-start(bf16[400,2048]{1,0:T(8,128)(2,1)} %param.6) | copy-start | bytes 4915204
  7.2 152.5 %all-gather.5.cloned.1.call-start = ((), (), s32[]{:S(2)}) async-start(), calls=%async_computation.3 | async-start | bytes 3727360 | tf_op jit(solution)/shard_map/all_gather | solution.py:39
  7.9 294.5 %all-gather.3.cloned.1.call-start = ((), (), s32[]{:S(2)}) async-start(), calls=%async_computation.2 | async-start | bytes 3727360 | tf_op jit(solution)/shard_map/all_gather | solution.py:40
  8.7 1003.1 %reduce-scatter.7.cloned.1.call-start = ((), (), s32[]{:S(2)}) async-start(), calls=%async_computation.5 | async-start | bytes 3727360
  12.6 289.8 %copy-start.2 = (bf16[400,896]{1,0:T(8,128)(2,1)S(1)}, bf16[400,896]{1,0:T(8,128)(2,1)}, u32[]{:S(2)}) copy-start(bf16[400,896]{1,0:T(8,128)(2,1)} %param.7) | copy-start | bytes 2150404
  317.2 736.8 %reduce-scatter.5.cloned.1.call-start = ((), (), s32[]{:S(2)}) async-start(), calls=%async_computation.4 | async-start | bytes 1843200 | tf_op jit(solution)/shard_map/reduce_scatter | solution.py:29
  317.2 4.1 copy-start.1
  317.2 4.1 copy-start.3
Sparse Core Ops, SparseCore 0:
  11.0 148.7 all-gather.4
  162.7 139.7 all-gather.2
  317.3 694.4 reduce-scatter.6
  1015.3 38.6 reduce-scatter.4
where the time goes:
time: 1060 us
  waiting for transfers between devices  1010 us (95%)
  matrix products  20.8 us (2%)
  between operations  15.1 us (1%)
    unnamed x5, waiting for transfers between devices  689 us
    all_gather x1, waiting for transfers between devices, on_device(): lax.all_gather(w_gate, 'dp', axis=0, tiled=True)  147 us
    all_gather x1, waiting for transfers between devices, on_device(): lax.all_gather(w_up, 'dp', axis=0, tiled=True)  138 us
    reduce_scatter x1, waiting for transfers between devices, group_sum(): lax.psum_scatter(partial_value.astype(jnp.bfloat16), 'mp', scatter_dimens...  40.4 us
  transfers between devices with their start and end apart: 4, of which 4 were waited for; matrix products, arithmetic and copies ran while one was open for 2% of the time, Pallas kernels for 0%

commit v1 on v0

--- a/solution.py
+++ b/solution.py
@@ -37,7 +37,9 @@
     dev_count = lax.axis_size("dp")
     gate_full, up_full = (
         lax.all_gather(w_gate, "dp", axis=0, tiled=True),
-        lax.all_gather(w_up, "dp", axis=0, tiled=True),
+        jnp.concatenate(
+            lax.all_to_all(jnp.stack([w_up] * lax.axis_size("dp")), "dp", 0, 0), axis=0
+        ),
     )
     sent = send_counts[0]
     got = recv_counts[0]

time: 1060 us -> 995 us (0.939)
  waiting for transfers between devices: 1010 us -> 925 us
  starting transfers between devices: 0.16 us -> 19.2 us
    all_gather x1 -> x0, waiting for transfers between devices: 138 us -> none  [on_device(): lax.all_gather(w_up, 'dp', axis=0, tiled=True)]
    all_gather x1, waiting for transfers between devices: 147 us -> 198 us  [on_device(): lax.all_gather(w_gate, 'dp', axis=0, tiled=True)]
    all_to_all x0 -> x1, starting transfers between devices: none -> 19 us  [on_device(): lax.all_to_all(jnp.stack([w_up] * lax.axis_size('dp')), 'dp', 0, 0)]
    unnamed x5 -> x4, waiting for transfers between devices: 689 us -> 687 us
  transfers between devices with their start and end apart: 4 -> 4, of which waited for: 4 -> 3; matrix products, arithmetic and copies ran while one was open for 2% -> 2% of each run, Pallas kernels for 0% -> 0%
where the time goes in v1:
time: 995 us; the launch traced here: 994 us
  waiting for transfers between devices  925 us (93%)
  matrix products  22.8 us (2%)
  starting transfers between devices  19.2 us (2%)
  between operations  15.1 us (2%)
  local copies, waits for them, and re-layouts  11 us (1%)
    unnamed x4, waiting for transfers between devices  687 us
    all_gather x1, waiting for transfers between devices, on_device(): lax.all_gather(w_gate, 'dp', axis=0, tiled=True)  198 us
    reduce_scatter x1, waiting for transfers between devices, group_sum(): lax.psum_scatter(partial_value.astype(jnp.bfloat16), 'mp', scatter_dimens...  40.5 us
  transfers between devices with their start and end apart: 4, of which 3 were waited for; matrix products, arithmetic and copies ran while one was open for 2% of the time, Pallas kernels for 0%

profile of v1, /device:TPU:8, one launch (start us, length us, event | category | flops | bytes accessed | tf_op | source)
XLA Modules:
  0.0 994.3 jit_solution(2987062269486212313)
XLA Ops:
  7.2 0.0 copy-start
  7.2 3.1 stack.2
  10.3 19.0 %all-to-all-start = ((bf16[64,32,896]{2,1,0:T(8,128)(2,1)}), bf16[64,32,896]{2,1,0:T(8,128)(2,1)}, u32[]{:S(2)}, u32[]{:S(2)}) async-start(bf16[64,32,896]{2,1,0:T(8,128)(2,1)} %stack.2), calls=%async_computation | async-start | bytes 7340032 | tf_op jit(solution)/shard_map/all_to_all | solution.py:41
  29.3 0.0 all-gather.2.cloned.1.call-start
  29.4 0.7 all-gather.2.cloned.1.call-update
  30.1 0.0 reduce-scatter.7.cloned.1.call-start
  30.1 0.6 reduce_sum.19
  30.8 0.6 reduce_sum.18
  32.7 0.0 copy-start.1
  32.7 197.7 %all-gather.2.cloned.1.call-done = bf16[2048,896]{1,0:T(8,128)(2,1)} async-done(((bf16[32,896]{1,0:T(8,128)(2,1)}), bf16[2048,896]{1,0:T(8,128)(2,1)}) %all-gather.2.cloned.1.call-update) | async-done | bytes 3670032 | tf_op jit(solution)/shard_map/all_gather | solution.py:39
  230.5 5.0 fusion.11
  235.5 0.0 all-to-all-done
  235.5 4.6 select_convert_fusion
  240.1 4.0 convert_bitcast_fusion
  244.1 6.1 copy.10
  250.2 0.0 reduce-scatter.7.cloned.1.call-update
  250.2 0.0 reduce-scatter.5.cloned.1.call-start
  250.3 4.0 fusion.12
  254.3 5.2 add_convert_fusion
  259.6 0.0 reduce-scatter.5.cloned.1.call-update
  259.6 685.8 %reduce-scatter.7.cloned.1.call-done = bf16[32,896]{1,0:T(8,128)(2,1)} async-done(((bf16[2048,896]{1,0:T(8,128)(2,1)}), bf16[32,896]{1,0:T(8,128)(2,1)}) %reduce-scatter.7.cloned.1.call-update) | async-done | bytes 57360
  945.4 1.0 copy.11
  946.4 0.8 copy.9
  947.2 40.5 %reduce-scatter.5.cloned.1.call-done = bf16[400,256]{1,0:T(8,128)(2,1)} async-done(((bf16[400,2048]{1,0:T(8,128)(2,1)}), bf16[400,256]{1,0:T(8,128)(2,1)}) %reduce-scatter.5.cloned.1.call-update) | async-done | bytes 204816 | tf_op jit(solution)/shard_map/reduce_scatter | solution.py:29
  (9 shorter events, 0.0 us)
Async XLA Ops:
  7.2 223.3 %copy-start = (bf16[400,2048]{1,0:T(8,128)(2,1)S(1)}, bf16[400,2048]{1,0:T(8,128)(2,1)}, u32[]{:S(2)}) copy-start(bf16[400,2048]{1,0:T(8,128)(2,1)} %param.6) | copy-start | bytes 4915204
  10.3 19.8 %copy-start.2 = (s32[1,64]{1,0:T(1,128)S(1)}, s32[1,64]{1,0:T(1,128)}, u32[]{:S(2)}) copy-start(s32[1,64]{1,0:T(1,128)} %param.11) | copy-start | bytes 772
  10.3 20.5 %copy-start.3 = (s32[1,64]{1,0:T(1,128)S(1)}, s32[1,64]{1,0:T(1,128)}, u32[]{:S(2)}) copy-start(s32[1,64]{1,0:T(1,128)} %param.10) | copy-start | bytes 772
  10.3 225.2 %all-to-all-start = ((bf16[64,32,896]{2,1,0:T(8,128)(2,1)}), bf16[64,32,896]{2,1,0:T(8,128)(2,1)}, u32[]{:S(2)}, u32[]{:S(2)}) async-start(bf16[64,32,896]{2,1,0:T(8,128)(2,1)} %stack.2), calls=%async_computation | async-start | bytes 7340032 | tf_op jit(solution)/shard_map/all_to_all | solution.py:41
  29.3 201.1 %all-gather.2.cloned.1.call-start = ((), (), s32[]{:S(2)}) async-start(), calls=%async_computation.3 | async-start | bytes 3727360 | tf_op jit(solution)/shard_map/all_gather | solution.py:39
  30.1 915.3 %reduce-scatter.7.cloned.1.call-start = ((), (), s32[]{:S(2)}) async-start(), calls=%async_computation.5 | async-start | bytes 3727360
  32.7 202.8 %copy-start.1 = (bf16[400,896]{1,0:T(8,128)(2,1)S(1)}, bf16[400,896]{1,0:T(8,128)(2,1)}, u32[]{:S(2)}) copy-start(bf16[400,896]{1,0:T(8,128)(2,1)} %param.7) | copy-start | bytes 2150404
  250.2 737.5 %reduce-scatter.5.cloned.1.call-start = ((), (), s32[]{:S(2)}) async-start(), calls=%async_computation.4 | async-start | bytes 1843200 | tf_op jit(solution)/shard_map/reduce_scatter | solution.py:29
  250.3 4.0 copy-start.4
Sparse Core Ops, SparseCore 0:
  33.1 197.2 all-gather.1
  250.4 695.0 reduce-scatter.6
  949.1 38.5 reduce-scatter.4
